TPU v7x, 32 devices: a whole 2x2x4 slice. The times are simulated.
32 devices in a mesh: group: 2 (over x), feat: 16 (over z, y, core).
Axes of the slice: x: 2, y: 2, z: 4, core: 2. Of those that a mesh axis runs over, the one named last changes fastest.
Arguments:
- store_inputs: bfloat16 [2, 512, 2048], P(None, ('group', 'feat')), parts along dimension 1, may hold values from -6 to 6
- store_targets: bfloat16 [2, 512, 2048], P(None, ('group', 'feat')), parts along dimension 1, may hold values from -6 to 6
- row_ids: int32 [256], P(('group', 'feat')), parts along dimension 0, may hold values from 0 to 15
- enc_weight: bfloat16 [2, 2048, 16384], P(None, None, 'feat'), may hold values from -0.125 to 0.125
- enc_bias: float32 [2, 16384], P(None, 'feat'), may hold values from -3 to 3
- dec_weight: bfloat16 [3, 16384, 2048], P(None, 'feat'), may hold values from -0.046875 to 0.046875
Outputs:
- enc_grad: bfloat16 [4, 2048, 16384], P('group', None, 'feat'), parts along dimension 0
- bias_grad: float32 [4, 16384], P('group', 'feat'), parts along dimension 0
- dec_grad: bfloat16 [6, 16384, 2048], P('group', 'feat'), parts along dimension 0
There are 2 independent parts, one for each index of `group`. A program takes and returns all parts, laid end to end along the dimension named above; an argument that names none is the same for every part. Nothing has to cross between parts.
Inputs may be any that keep to these rules, and one draw needn't show every extreme that they name: row_ids[i] indexes the store rows held with token i, as in the first step.
All inputs are finite; a program needn't handle non-finite values.
Results may differ from a plain program's by a relative error of at most 0.035.
Values may be sent and summed in bfloat16 or wider, within the bound.
A program may use at most 128 MiB of HBM per device.

v0:
```python
import math

import jax
import jax.numpy as jnp
from jax import lax
from jax.sharding import PartitionSpec as P


def local(store_inputs, store_targets, row_ids, enc_weight, enc_bias, dec_weight):
    layers = enc_weight.shape[0]
    model_width = enc_weight.shape[1]
    tile_width = enc_weight.shape[2]
    local_rows = row_ids.shape[0]
    pair_list = [(source, target) for source in range(layers) for target in range(source, layers)]
    picked_in = (
        jnp.take(store_inputs, row_ids, axis=1)
        .transpose(1, 0, 2)
        .reshape(local_rows, layers * model_width)
    )
    picked_out = (
        jnp.take(store_targets, row_ids, axis=1)
        .transpose(1, 0, 2)
        .reshape(local_rows, layers * model_width)
    )
    inputs_all = lax.all_gather(picked_in, "feat", axis=0, tiled=True)
    tokens = inputs_all.shape[0]
    grad_scale = 1.0 / math.sqrt(tokens)
    layer_inputs = [
        inputs_all[:, index * model_width : (index + 1) * model_width] for index in range(layers)
    ]
    preact = [
        jnp.dot(layer_inputs[index], enc_weight[index], preferred_element_type=jnp.float32)
        + enc_bias[index]
        for index in range(layers)
    ]
    features = [jnp.maximum(value, 0.0).astype(jnp.bfloat16) for value in preact]

    def decoder_terms():
        part_features = [value for value in features]
        outputs = []
        for target in range(layers):
            rebuilt = jnp.zeros((local_rows * lax.axis_size("feat"), model_width), jnp.float32)
            for index, (source, goal) in enumerate(pair_list):
                if goal == target:
                    rebuilt = rebuilt + jnp.dot(
                        part_features[source], dec_weight[index], preferred_element_type=jnp.float32
                    )
            outputs.append(rebuilt)
        return jnp.concatenate(outputs, axis=1)

    def backward_step(block_rows):
        row_count = block_rows.shape[0]
        part_features = [value for value in features]
        part_preact = [value for value in preact]
        part_errors = [
            block_rows[:, index * model_width : (index + 1) * model_width]
            for index in range(layers)
        ]
        feature_grad = [jnp.zeros((row_count, tile_width), jnp.float32) for index in range(layers)]
        updated = []
        for index, (source, target) in enumerate(pair_list):
            product = lax.dot_general(
                part_features[source],
                part_errors[target],
                (((0,), (0,)), ((), ())),
                preferred_element_type=jnp.float32,
            )
            updated.append(product)
            feature_grad[source] = feature_grad[source] + lax.dot_general(
                part_errors[target],
                dec_weight[index],
                (((1,), (1,)), ((), ())),
                preferred_element_type=jnp.float32,
            )
        pre_rows = jnp.stack(
            [
                jnp.where(part_preact[index] > 0, feature_grad[index], 0.0) * grad_scale
                for index in range(layers)
            ]
        )
        return (tuple(updated), pre_rows)

    rebuilt_own = lax.psum_scatter(decoder_terms(), "feat", scatter_dimension=0, tiled=True)
    errors_own = (rebuilt_own - picked_out.astype(jnp.float32)).astype(jnp.bfloat16)
    gradients, pre_buffer = backward_step(lax.all_gather(errors_own, "feat", axis=0, tiled=True))
    dec_grad = jnp.stack([(grad_scale * value).astype(jnp.bfloat16) for value in gradients])
    bias_grad = jnp.sum(pre_buffer, axis=1)
    pre_half = pre_buffer.astype(jnp.bfloat16)
    enc_grad = jnp.stack(
        [
            lax.dot_general(
                layer_inputs[index],
                pre_half[index],
                (((0,), (0,)), ((), ())),
                preferred_element_type=jnp.float32,
            ).astype(jnp.bfloat16)
            for index in range(layers)
        ]
    )
    return (enc_grad, bias_grad, dec_grad)


def solution(mesh):
    in_specs = (
        P(None, ("group", "feat"), None),
        P(None, ("group", "feat"), None),
        P(("group", "feat")),
        P(None, None, "feat"),
        P(None, "feat"),
        P(None, "feat", None),
    )
    out_specs = (P("group", None, "feat"), P("group", "feat"), P("group", "feat", None))
    return jax.shard_map(local, mesh=mesh, in_specs=in_specs, out_specs=out_specs, check_vma=False)
```

profile of v0, /device:TPU:0, one launch (start us, length us, event | category | flops | bytes accessed | tf_op | source)
XLA Modules:
  0.0 205.0 jit_solution(16663511972218497202)
XLA Ops:
  7.2 0.0 copy-start
  7.2 0.0 all-gather.3.cloned.1.call-start
  7.2 0.7 compare_select_fusion
  7.9 0.7 compare_and_fusion
  8.6 0.0 copy-done
  8.6 0.7 gather_fusion
  9.3 1.6 gather_fusion.1
  11.0 0.7 bitcast_convert_fusion
  11.7 0.0 all-gather.3.cloned.1.call-update
  11.7 0.0 reduce-scatter.2.cloned.1.call-start
  11.8 0.8 fusion.71
  12.6 39.9 %all-gather.3.cloned.1.call-done = bf16[128,4096]{1,0:T(8,128)(2,1)} async-done(((bf16[8,4096]{1,0:T(8,128)(2,1)}), bf16[128,4096]{1,0:T(8,128)(2,1)}) %all-gather.3.cloned.1.call-update) | async-done | bytes 1048592 | tf_op jit(solution)/shard_map/all_gather | solution.py:25
  52.5 0.0 copy-start.2
  52.5 0.0 copy-start.3
  52.5 3.2 %fusion.36 = f32[128,1024]{1,0:T(8,128)S(1)} fusion(bf16[2,2048,1024]{2,1,0:T(8,128)(2,1)} %param.11, bf16[128,4096]{1,0:T(8,128)(2,1)} %all-gather.3.cloned.1.call-done, f32[1024]{0:T(1024)S(1)} %bitcast.81), kind=kOutput, calls=%fused_computation.40 | convolution fusion | flops 537001984 | bytes 5246976 | tf_op jit(solution)/shard_map/dot_general | solution.py:32
  55.7 3.7 %fusion.2 = f32[128,2048]{1,0:T(8,128)S(1)} fusion(bf16[3,1024,2048]{2,1,0:T(8,128)(2,1)} %param.13, f32[128,1024]{1,0:T(8,128)S(1)} %fusion.36), kind=kOutput, calls=%fused_computation.9 | convolution fusion | flops 537133056 | bytes 5767168 | tf_op jit(solution)/shard_map/dot_general | solution.py:45
  59.4 0.0 copy-done.2
  59.4 2.9 %maximum_convert_fusion.1 = (bf16[128,1024]{1,0:T(8,128)(2,1)S(1)}, f32[128,1024]{1,0:T(8,128)S(1)}) fusion(f32[1024]{0:T(1024)S(1)} %bitcast.80, bf16[2,2048,1024]{2,1,0:T(8,128)(2,1)} %param.11, bf16[128,4096]{1,0:T(8,128)(2,1)S(1)} %copy-done.2), kind=kOutput, calls=%fused_computation.51 | convolution fusion | flops 537264128 | bytes 5509120 | tf_op jit(solution)/shard_map/dot_general | solution.py:32
  62.3 0.0 copy-done.3
  62.3 0.7 fusion.12
  63.0 0.8 fusion.27
  63.8 1.5 pad_maximum_fusion.2
  65.3 0.0 reduce-scatter.2.cloned.1.call-update
  65.3 0.2 all-gather.5.cloned.1.call-start
  65.5 60.7 %reduce-scatter.2.cloned.1.call-done = f32[8,4096]{1,0:T(8,128)} async-done(((f32[128,4096]{1,0:T(8,128)}), f32[8,4096]{1,0:T(8,128)}) %reduce-scatter.2.cloned.1.call-update) | async-done | bytes 131088 | tf_op jit(solution)/shard_map/reduce_scatter | solution.py:83
  126.2 1.5 subtract_convert_fusion
  127.8 0.0 all-gather.5.cloned.1.call-update
  127.8 38.0 %all-gather.5.cloned.1.call-done = bf16[128,4096]{1,0:T(8,128)(2,1)} async-done(((bf16[8,4096]{1,0:T(8,128)(2,1)}), bf16[128,4096]{1,0:T(8,128)(2,1)}) %all-gather.5.cloned.1.call-update) | async-done | bytes 1048592 | tf_op jit(solution)/shard_map/all_gather | solution.py:85
  165.8 0.0 copy-start.4
  165.8 3.9 %fusion.6 = f32[128,1024]{1,0:T(8,128)S(1)} fusion(bf16[3,1024,2048]{2,1,0:T(8,128)(2,1)} %param.13, bf16[128,4096]{1,0:T(8,128)(2,1)} %all-gather.5.cloned.1.call-done), kind=kOutput, calls=%fused_computation.13 | convolution fusion | flops 536870912 | bytes 5242880 | tf_op jit(solution)/shard_map/dot_general | solution.py:69
  169.8 3.9 %fusion.54 = f32[1,128,1024]{2,1,0:T(8,128)S(1)} fusion(bf16[3,1024,2048]{2,1,0:T(8,128)(2,1)} %param.13, f32[128,1024]{1,0:T(8,128)S(1)} %fusion.36, bf16[128,4096]{1,0:T(8,128)(2,1)} %all-gather.5.cloned.1.call-done), kind=kOutput, calls=%fused_computation.46 | convolution fusion | flops 537264128 | bytes 5767168 | tf_op jit(solution)/shard_map/dot_general | solution.py:69
  173.7 0.0 copy-done.4
  173.7 3.8 %fusion.45 = f32[1,128,1024]{2,1,0:T(8,128)S(1)} fusion(f32[128,1024]{1,0:T(8,128)S(1)} %fusion.6, bf16[3,1024,2048]{2,1,0:T(8,128)(2,1)} %param.13, f32[128,1024]{1,0:T(8,128)S(1)} %get-tuple-element.9, bf16[128,4096]{1,0:T(8,128)(2,1)S(1)} %copy-done.4), kind=kOutput, calls=%fused_computation.43 | convolution fusion | flops 537395200 | bytes 6291456 | tf_op jit(solution)/shard_map/dot_general | solution.py:69
  177.5 0.1 fusion.58
  177.5 0.7 fusion.57
  178.2 1.3 convert_bitcast_fusion.1
  179.5 3.3 %convert_bitcast_fusion = bf16[1,2048,1024]{2,1,0:T(8,128)(2,1)} fusion(bf16[128,4096]{1,0:T(8,128)(2,1)S(1)} %copy-done.2, bf16[2,128,1024]{2,1,0:T(8,128)(2,1)S(1)} %fusion.58), kind=kOutput, calls=%fused_computation.23 | convolution fusion | flops 538968064 | bytes 4980736 | tf_op jit(solution)/shard_map/dot_general | solution.py:91
  182.8 0.0 copy-start.5
  182.8 6.4 %pad_maximum_fusion.1 = bf16[2,2048,1024]{2,1,0:T(8,128)(2,1)} fusion(bf16[1,2048,1024]{2,1,0:T(8,128)(2,1)} %convert_bitcast_fusion, bf16[1,2048,1024]{2,1,0:T(8,128)(2,1)S(1)} %convert_bitcast_fusion.1), kind=kLoop, calls=%fused_computation.3 | loop fusion | flops 4194304 | bytes 16777216 | tf_op jit(solution)/shard_map/stack | solution.py:89
  189.2 0.0 copy-done.5
  189.2 1.3 fusion.24
  190.5 1.3 fusion.25
  191.8 0.0 copy-start.1
  191.8 1.3 fusion.26
  193.1 5.4 %pad_maximum_fusion = bf16[3,1024,2048]{2,1,0:T(8,128)(2,1)} fusion(bf16[1,1024,2048]{2,1,0:T(8,128)(2,1)S(1)} %fusion.26, bf16[1,1024,2048]{2,1,0:T(8,128)(2,1)S(1)} %fusion.25, bf16[1,1024,2048]{2,1,0:T(8,128)(2,1)S(1)} %fusion.24), kind=kLoop, calls=%fused_computation.2 | loop fusion | flops 12582912 | bytes 25165824 | tf_op jit(solution)/shard_map/stack | solution.py:86
  198.4 0.0 copy-done.1
  (1 shorter events, 0.0 us)
Async XLA Ops:
  7.2 1.4 copy-start
  7.2 45.3 %all-gather.3.cloned.1.call-start = ((), (), s32[]{:S(2)}) async-start(), calls=%async_computation.1 | async-start | bytes 1114112 | tf_op jit(solution)/shard_map/all_gather | solution.py:25
  11.7 114.5 %reduce-scatter.2.cloned.1.call-start = ((), (), s32[]{:S(2)}) async-start(), calls=%async_computation.2 | async-start | bytes 2228224 | tf_op jit(solution)/shard_map/reduce_scatter | solution.py:83
  52.5 6.9 %copy-start.2 = (bf16[128,4096]{1,0:T(8,128)(2,1)S(1)}, bf16[128,4096]{1,0:T(8,128)(2,1)}, u32[]{:S(2)}) copy-start(bf16[128,4096]{1,0:T(8,128)(2,1)} %all-gather.3.cloned.1.call-done) | copy-start | bytes 3145732
  52.5 9.8 %copy-start.3 = (bf16[3,1024,2048]{2,1,0:T(8,128)(2,1)S(1)}, bf16[3,1024,2048]{2,1,0:T(8,128)(2,1)}, u32[]{:S(2)}) copy-start(bf16[3,1024,2048]{2,1,0:T(8,128)(2,1)} %param.13) | copy-start | bytes 37748740
  65.3 100.5 %all-gather.5.cloned.1.call-start = ((), (), s32[]{:S(2)}) async-start(), calls=%async_computation.3 | async-start | bytes 1114112 | tf_op jit(solution)/shard_map/all_gather | solution.py:85
  165.8 7.9 %copy-start.4 = (bf16[128,4096]{1,0:T(8,128)(2,1)S(1)}, bf16[128,4096]{1,0:T(8,128)(2,1)}, u32[]{:S(2)}) copy-start(bf16[128,4096]{1,0:T(8,128)(2,1)} %all-gather.5.cloned.1.call-done) | copy-start | bytes 3145732
  182.8 6.4 %copy-start.5 = (bf16[128,4096]{1,0:T(8,128)(2,1)S(1)}, bf16[128,4096]{1,0:T(8,128)(2,1)}, u32[]{:S(2)}) copy-start(bf16[128,4096]{1,0:T(8,128)(2,1)} %all-gather.5.cloned.1.call-done) | copy-start | bytes 3145732
  191.8 6.7 %copy-start.1 = (bf16[2,16,2048]{2,1,0:T(8,128)(2,1)S(1)}, bf16[2,16,2048]{2,1,0:T(8,128)(2,1)}, u32[]{:S(2)}) copy-start(bf16[2,16,2048]{2,1,0:T(8,128)(2,1)} %param.8) | copy-start | bytes 393220
Sparse Core Ops, SparseCore 0:
  11.9 40.5 all-gather.2
  65.4 60.7 reduce-scatter.1
  129.0 36.7 all-gather.4
where the time goes:
time: 205 us
  waiting for transfers between devices  139 us (68%)
  matrix products  31.2 us (15%)
  other arithmetic  17.6 us (9%)
  between operations  13.9 us (7%)
  local copies, waits for them, and re-layouts  3.21 us (2%)
    reduce_scatter x1, waiting for transfers between devices, local(): lax.psum_scatter(decoder_terms(), 'feat', scatter_dimension=0, tiled=True)  60.7 us
    all_gather x1, waiting for transfers between devices, local(): inputs_all = lax.all_gather(picked_in, 'feat', axis=0, tiled=True)  39.9 us
    all_gather x1, waiting for transfers between devices, local(): lax.all_gather(errors_own, 'feat', axis=0, tiled=True)  38 us
    dot_general x3, matrix products, backward_step(): lax.dot_general(part_errors[target], dec_weight[index], (((1,), (1,)), ((...  11.6 us
    another operation x1, other arithmetic, local(): jnp.stack([lax.dot_general(layer_inputs[index], pre_half[index], (((0,),...  6.44 us
    dot_general x2, matrix products, local(): jnp.dot(layer_inputs[index], enc_weight[index], preferred_element_type=jn...  6.12 us
    another operation x1, other arithmetic, local(): jnp.stack([(grad_scale * value).astype(jnp.bfloat16) for value in gradien...  5.38 us
    dot_general x3, matrix products, decoder_terms(): jnp.dot(part_features[source], dec_weight[index], preferred_element_type=...  5.14 us
  transfers between devices with their start and end apart: 3, of which 3 were waited for; matrix products, arithmetic and copies ran while one was open for 0% of the time, Pallas kernels for 0%

commit v1 on v0

v1 whole, which is shorter than its diff:
```python
import functools
import math

import jax
import jax.numpy as jnp
from jax import lax
from jax.experimental import pallas as pl
from jax.experimental.pallas import tpu as pltpu
from jax.sharding import PartitionSpec as P

BF = jnp.bfloat16
F32 = jnp.float32


def place(n):
    me = lax.axis_index("feat")
    return me // 4, (me // 2) % 2, me % 2


def index_of(z, y, c):
    return (z * 2 + y) * 2 + c


def near_first(depth):
    return sorted(range(1, depth), key=lambda k: min(k, depth - k))


def greet(n):
    depth = n // 4
    z, y, c = place(n)
    barrier = pltpu.get_barrier_semaphore()
    peers = [index_of(z, y, 1 - c), index_of(z, 1 - y, c)]
    peers += [index_of((z + k) % depth, y, c) for k in range(1, depth)]
    for peer in peers:
        pl.semaphore_signal(
            barrier, inc=1, device_id={"feat": peer}, device_id_type=pl.DeviceIdType.MESH
        )
    pl.semaphore_wait(barrier, len(peers))


def send(src, dst, send_sem, recv_sem, peer):
    return pltpu.make_async_remote_copy(
        src_ref=src,
        dst_ref=dst,
        send_sem=send_sem,
        recv_sem=recv_sem,
        device_id={"feat": peer},
        device_id_type=pl.DeviceIdType.MESH,
    )


def spread(n, buf, zs, zr, ys, yr, cs, cr):
    depth = n // 4
    z, y, c = place(n)
    core, side = index_of(z, y, 1 - c), index_of(z, 1 - y, c)
    started = []

    def go(chunk, send_sem, recv_sem, peer):
        copy = send(buf.at[chunk], buf.at[chunk], send_sem, recv_sem, peer)
        copy.start()
        started.append(copy)

    def arrive(chunk, send_sem, recv_sem, peer):
        send(buf.at[chunk], buf.at[chunk], send_sem, recv_sem, peer).wait_recv()

    order = near_first(depth)
    mine = index_of(z, y, c)
    go(mine, ys.at[0], yr.at[0], side)
    for k in reversed(order):
        go(mine, zs.at[k], zr.at[k], index_of((z + k) % depth, y, c))
    go(mine, cs.at[0], cr.at[0], core)
    for k in order:
        chunk = index_of((z - k + depth) % depth, y, c)
        arrive(chunk, zs.at[k], zr.at[k], core)
        go(chunk, ys.at[k], yr.at[k], side)
        go(chunk, cs.at[k], cr.at[k], core)
    for k in [0] + order:
        chunk = index_of((z - k + depth) % depth, 1 - y, c)
        arrive(chunk, ys.at[k], yr.at[k], side)
        go(chunk, cs.at[depth + k], cr.at[depth + k], core)
    for k in [0] + order:
        arrive(index_of((z - k + depth) % depth, y, 1 - c), cs.at[k], cr.at[k], core)
    for k in [0] + order:
        chunk = index_of((z - k + depth) % depth, 1 - y, 1 - c)
        arrive(chunk, cs.at[depth + k], cr.at[depth + k], core)
    for copy in started:
        copy.wait_send()


def gathered(n, layers, buf, out_ref):
    rows = buf.shape[1]
    width = out_ref.shape[2]
    for i in range(0, n, 2):
        for layer in range(layers):
            cols = pl.ds(layer * width, width)
            both = jnp.concatenate([buf[i, :, cols].astype(F32), buf[i + 1, :, cols].astype(F32)])
            out_ref[layer, pl.ds(i * rows, 2 * rows), :] = both.astype(BF)


def gather_kernel(n, layers, ids_ref, store_ref, out_ref, buf, *sems):
    width = store_ref.shape[2]
    me = lax.axis_index("feat")
    held = store_ref.shape[1]
    rows = ids_ref.shape[0]
    hot = (ids_ref[...] == lax.broadcasted_iota(jnp.int32, (rows, held), 1)).astype(BF)
    for layer in range(layers):
        picked = jnp.dot(hot, store_ref[layer], preferred_element_type=F32)
        buf[me, :, pl.ds(layer * width, width)] = picked.astype(BF)
    greet(n)
    spread(n, buf, *sems)
    gathered(n, layers, buf, out_ref)


def errors_kernel(
    n, layers, ids_ref, store_ref, part_ref, out_ref, buf, cst, yst, zst, cin, yin, zin,
    rcs, rcr, rys, ryr, rzs, rzr, *sems
):
    depth = n // 4
    width = store_ref.shape[2]
    held = store_ref.shape[1]
    rows = ids_ref.shape[0]
    z, y, c = place(n)
    core, side = index_of(z, y, 1 - c), index_of(z, 1 - y, c)
    order = near_first(depth)
    far = list(reversed(order)) + [0]
    started = []
    greet(n)

    def go(src, dst, send_sem, recv_sem, peer):
        copy = send(src, dst, send_sem, recv_sem, peer)
        copy.start()
        started.append(copy)

    def term(zz, yy, cc):
        index = index_of(zz, yy, cc)
        return [part_ref[layer, index] for layer in range(layers)]

    def keep(dst, slot, values):
        for layer in range(layers):
            dst[slot, :, pl.ds(layer * width, width)] = values[layer].astype(BF)

    def plus(values, src, slot):
        return [
            values[layer] + src[slot, :, pl.ds(layer * width, width)].astype(F32)
            for layer in range(layers)
        ]

    for j, yy in ((0, 1 - y), (1, y)):
        for k in far:
            slot = j * depth + k
            keep(cst, slot, term((z + k) % depth, yy, 1 - c))
            go(cst.at[slot], cin.at[slot], rcs.at[slot], rcr.at[slot], core)
    for k in far:
        send(cst.at[k], cin.at[k], rcs.at[k], rcr.at[k], core).wait_recv()
        keep(yst, k, plus(term((z + k) % depth, 1 - y, c), cin, k))
        go(yst.at[k], yin.at[k], rys.at[k], ryr.at[k], side)
    hot = (ids_ref[...] == lax.broadcasted_iota(jnp.int32, (rows, held), 1)).astype(BF)
    targets = [jnp.dot(hot, store_ref[layer], preferred_element_type=F32) for layer in range(layers)]
    for k in far:
        slot = depth + k
        send(cst.at[slot], cin.at[slot], rcs.at[slot], rcr.at[slot], core).wait_recv()
        send(yst.at[k], yin.at[k], rys.at[k], ryr.at[k], side).wait_recv()
        total = plus(plus(term((z + k) % depth, y, c), cin, slot), yin, k)
        if k:
            keep(zst, k, total)
            go(zst.at[k], zin.at[k], rzs.at[k], rzr.at[k], index_of((z + k) % depth, y, c))
    for k in order:
        send(zst.at[k], zin.at[k], rzs.at[k], rzr.at[k], core).wait_recv()
        total = plus(total, zin, k)
    keep(buf, index_of(z, y, c), [total[layer] - targets[layer] for layer in range(layers)])
    for copy in started:
        copy.wait_send()
    spread(n, buf, *sems)
    gathered(n, layers, buf, out_ref)


def gather_sems(depth):
    dma = pltpu.SemaphoreType.DMA
    return [dma((depth,))] * 4 + [dma((2 * depth,))] * 2


VMEM = pl.BlockSpec(memory_space=pltpu.VMEM)


def gather_inputs(n, ids, store):
    layers, _, width = store.shape
    rows = ids.shape[0]
    return pl.pallas_call(
        functools.partial(gather_kernel, n, layers),
        out_shape=jax.ShapeDtypeStruct((layers, n * rows, width), BF),
        in_specs=[VMEM] * 2,
        out_specs=VMEM,
        scratch_shapes=[pltpu.VMEM((n, rows, layers * width), BF)] + gather_sems(n // 4),
        compiler_params=pltpu.CompilerParams(collective_id=0, has_side_effects=True),
        name="gather_inputs",
    )(ids, store)


def reduce_errors(n, ids, store, part):
    layers, _, width = store.shape
    rows = ids.shape[0]
    depth = n // 4
    dma = pltpu.SemaphoreType.DMA
    chunks = lambda count: pltpu.VMEM((count, rows, layers * width), BF)
    return pl.pallas_call(
        functools.partial(errors_kernel, n, layers),
        out_shape=jax.ShapeDtypeStruct((layers, n * rows, width), BF),
        in_specs=[VMEM] * 3,
        out_specs=VMEM,
        scratch_shapes=[chunks(n), chunks(2 * depth), chunks(depth), chunks(depth)]
        + [chunks(2 * depth), chunks(depth), chunks(depth)]
        + [dma((2 * depth,))] * 2
        + [dma((depth,))] * 4
        + gather_sems(depth),
        compiler_params=pltpu.CompilerParams(collective_id=1, has_side_effects=True),
        name="reduce_errors",
    )(ids, store, part)


def backward_kernel(pairs, scale, x_ref, e_ref, a_ref, w_ref, enc_ref, bias_ref, dec_ref, xt):
    layers = x_ref.shape[0]

    @pl.when(pl.program_id(0) == 0)
    def _():
        for layer in range(layers):
            xt[layer] = x_ref[layer].T

    for source in range(layers):
        active = a_ref[source]
        turned = jnp.maximum(active, 0.0).astype(BF).T
        grad = None
        for index, (first, target) in enumerate(pairs):
            if first != source:
                continue
            dec = jnp.dot(turned, e_ref[target], preferred_element_type=F32)
            dec_ref[index] = (scale * dec).astype(BF)
            back = lax.dot_general(
                e_ref[target], w_ref[index], (((1,), (1,)), ((), ())), preferred_element_type=F32
            )
            grad = back if grad is None else grad + back
        pre = jnp.where(active > 0, grad, 0.0) * scale
        bias_ref[pl.ds(source, 1), :] = jnp.sum(pre, axis=0, keepdims=True)
        enc = jnp.dot(xt[source], pre.astype(BF), preferred_element_type=F32)
        enc_ref[source] = enc.astype(BF)


def backward(pairs, scale, x, errors, preact, dec_weight):
    layers, tokens, width = x.shape
    features = preact.shape[2]
    tile = min(256, features)
    whole = pl.BlockSpec((layers, tokens, width), lambda i: (0, 0, 0))
    rows = pl.BlockSpec((len(pairs), tile, width), lambda i: (0, i, 0))
    return pl.pallas_call(
        functools.partial(backward_kernel, pairs, scale),
        grid=(features // tile,),
        out_shape=(
            jax.ShapeDtypeStruct((layers, width, features), BF),
            jax.ShapeDtypeStruct((layers, features), F32),
            jax.ShapeDtypeStruct((len(pairs), features, width), BF),
        ),
        in_specs=[whole, whole, pl.BlockSpec((layers, tokens, tile), lambda i: (0, 0, i)), rows],
        out_specs=(
            pl.BlockSpec((layers, width, tile), lambda i: (0, 0, i)),
            pl.BlockSpec((layers, tile), lambda i: (0, i)),
            rows,
        ),
        scratch_shapes=[pltpu.VMEM((layers, width, tokens), BF)],
        compiler_params=pltpu.CompilerParams(vmem_limit_bytes=48 * 1024 * 1024),
        name="backward",
    )(x, errors, preact, dec_weight)


def local(n, store_inputs, store_targets, row_ids, enc_weight, enc_bias, dec_weight):
    layers, width = enc_weight.shape[:2]
    rows = row_ids.shape[0]
    pairs = [(source, target) for source in range(layers) for target in range(source, layers)]
    scale = 1.0 / math.sqrt(rows * n)
    ids = row_ids.reshape(rows, 1)
    x = gather_inputs(n, ids, store_inputs)
    preact = [
        jnp.dot(x[layer], enc_weight[layer], preferred_element_type=F32) + enc_bias[layer]
        for layer in range(layers)
    ]
    features = [jnp.maximum(value, 0.0).astype(BF) for value in preact]
    part = []
    for target in range(layers):
        part.append(
            sum(
                jnp.dot(features[source], dec_weight[index], preferred_element_type=F32)
                for index, (source, goal) in enumerate(pairs)
                if goal == target
            )
        )
    part = jnp.stack(part).reshape(layers, n, rows, width)
    errors = reduce_errors(n, ids, store_targets, part)
    return backward(pairs, scale, x, errors, jnp.stack(preact), dec_weight)


def solution(mesh):
    in_specs = (
        P(None, ("group", "feat"), None),
        P(None, ("group", "feat"), None),
        P(("group", "feat")),
        P(None, None, "feat"),
        P(None, "feat"),
        P(None, "feat", None),
    )
    out_specs = (P("group", None, "feat"), P("group", "feat"), P("group", "feat", None))
    body = functools.partial(local, mesh.shape["feat"])
    return jax.shard_map(body, mesh=mesh, in_specs=in_specs, out_specs=out_specs, check_vma=False)
```

time: 205 us -> 84.2 us (0.41)
  waiting for transfers between devices: 139 us -> 0 us
  Pallas kernels: 0 us -> 68.7 us
  matrix products: 31.2 us -> 9.02 us
  other arithmetic: 17.6 us -> 1.53 us
  between operations: 13.9 us -> 0.73 us
    all_gather x2 -> x0, waiting for transfers between devices: 77.9 us -> none  [the longest x1 39.9 us: local(): inputs_all = lax.all_gather(picked_in, 'feat', axis=0, tiled=True)]
    pallas_call x0 -> x3, Pallas kernels: none -> 68.7 us  [the longest x1 29.4 us: reduce_errors(): pl.pallas_call(functools.partial(errors_kernel, n, layers), out_shape=jax...]
    reduce_scatter x1 -> x0, waiting for transfers between devices: 60.7 us -> none  [local(): lax.psum_scatter(decoder_terms(), 'feat', scatter_dimension=0, tiled=True)]
    dot_general x13 -> x5, matrix products: 31.2 us -> 9.02 us  [the longest x2 6.8 us: local(): jnp.dot(x[layer], enc_weight[layer], preferred_element_type=F32)]
    another operation x2, other arithmetic: 11.8 us -> 1.53 us  [the longest x1 1.46 us: local(): part = jnp.stack(part).reshape(layers, n, rows, width)]
    gather x2 -> x0, local copies, waits for them, and re-layouts: 2.39 us -> none  [the longest x1 1.65 us: local(): jnp.take(store_targets, row_ids, axis=1).transpose(1, 0, 2)]
    convert_element_type x3 -> x0, other arithmetic: 2.33 us -> none  [the longest x1 1.55 us: local(): (rebuilt_own - picked_out.astype(jnp.float32)).astype(jnp.bfloat16)]
  transfers between devices with their start and end apart: 3 -> 0, of which waited for: 3 -> 0; matrix products, arithmetic and copies ran while one was open for 0% -> 0% of each run, Pallas kernels for 0% -> 0%
where the time goes in v1:
time: 84.2 us; the launch traced here: 83.8 us
  Pallas kernels  68.7 us (82%)
  matrix products  9.02 us (11%)
  local copies, waits for them, and re-layouts  3.84 us (5%)
  other arithmetic  1.53 us (2%)
    pallas_call x1, Pallas kernels, reduce_errors(): pl.pallas_call(functools.partial(errors_kernel, n, layers), out_shape=jax...  29.4 us
    pallas_call x1, Pallas kernels, gather_inputs(): pl.pallas_call(functools.partial(gather_kernel, n, layers), out_shape=jax...  20 us
    pallas_call x1, Pallas kernels, backward(): pl.pallas_call(functools.partial(backward_kernel, pairs, scale), grid=(fe...  19.3 us
    dot_general x2, matrix products, local(): jnp.dot(x[layer], enc_weight[layer], preferred_element_type=F32)  6.8 us
    dot_general x3, matrix products, local(): jnp.dot(features[source], dec_weight[index], preferred_element_type=F32)  2.21 us
    unnamed x6, local copies, waits for them, and re-layouts  1.73 us

profile of v1, /device:TPU:0, one launch (start us, length us, event | category | flops | bytes accessed | tf_op | source)
XLA Modules:
  0.0 83.8 jit_solution(829868714653386980)
XLA Ops:
  0.6 1.3 %copy.9.ids_ref = s32[8,1]{1,0:T(8,128)} copy(s32[8,1]{0,1:T(1,128)} %bitcast.48) | data formatting | bytes 64 | tf_op jit(solution)/shard_map/reshape | solution.py:278
  2.0 0.8 fusion.39
  2.7 20.0 %gather_inputs.1.x_ref = bf16[2,128,2048]{2,1,0:T(8,128)(2,1)} custom-call(s32[8,1]{1,0:T(8,128)} %copy.9.ids_ref, bf16[2,16,2048]{2,1,0:T(8,128)(2,1)} %store_ref.2), custom_call_target="tpu_custom_call" | custom-call | tf_op jit(solution)/shard_map/gather_inputs/pallas_call | solution.py:188
  22.8 0.0 copy-start.2
  22.8 3.2 %fusion.24 = f32[128,1024]{1,0:T(8,128)S(1)} fusion(bf16[2,2048,1024]{2,1,0:T(8,128)(2,1)} %param.9, bf16[2,128,2048]{2,1,0:T(8,128)(2,1)} %gather_inputs.1.x_ref, f32[1024]{0:T(1024)S(1)} %bitcast.47), kind=kOutput, calls=%fused_computation.19 | convolution fusion | flops 537001984 | bytes 5246976 | tf_op jit(solution)/shard_map/dot_general | solution.py:281
  26.0 3.6 %fusion.27 = f32[128,1024]{1,0:T(8,128)S(1)} fusion(bf16[2,2048,1024]{2,1,0:T(8,128)(2,1)} %param.9, bf16[2,128,2048]{2,1,0:T(8,128)(2,1)} %gather_inputs.1.x_ref, f32[1024]{0:T(1024)S(1)} %bitcast.46), kind=kOutput, calls=%fused_computation.20 | convolution fusion | flops 537001984 | bytes 5246976 | tf_op jit(solution)/shard_map/dot_general | solution.py:281
  29.6 0.1 pad_maximum_fusion.1.a_ref
  29.7 0.5 copy-done.2
  30.2 0.7 fusion
  30.9 0.7 fusion.21
  31.7 0.0 copy-start
  31.7 0.8 fusion.15
  32.5 1.5 %pad_maximum_fusion.part_ref = f32[2,16,8,2048]{3,2,1,0:T(8,128)} fusion(f32[1,16,8,2048]{3,2,1,0:T(8,128)S(1)} %fusion.21, f32[1,16,8,2048]{3,2,1,0:T(8,128)S(1)} %fusion.15), kind=kLoop, calls=%fused_computation.18 | loop fusion | flops 524288 | bytes 4194304 | tf_op jit(solution)/shard_map/stack | solution.py:294
  33.9 29.4 %reduce_errors.1.e_ref = bf16[2,128,2048]{2,1,0:T(8,128)(2,1)} custom-call(s32[8,1]{1,0:T(8,128)} %copy.9.ids_ref, bf16[2,16,2048]{2,1,0:T(8,128)(2,1)} %store_ref.3, f32[2,16,8,2048]{3,2,1,0:T(8,128)} %pad_maximum_fusion.part_ref), custom_call_target="tpu_custom_call" | custom-call | tf_op jit(solution)/shard_map/reduce_errors/pallas_call | solution.py:205
  63.3 0.0 copy-done
  63.3 0.0 copy-start.1
  63.3 1.2 %copy-done.1 = bf16[2,128,2048]{2,1,0:T(8,128)(2,1)S(1)} copy-done((bf16[2,128,2048]{2,1,0:T(8,128)(2,1)S(1)}, bf16[2,128,2048]{2,1,0:T(8,128)(2,1)}, u32[]{:S(2)}) %copy-start.1) | copy-done | bytes 1048600
  64.5 19.3 %backward.1 = (bf16[2,2048,1024]{2,1,0:T(8,128)(2,1)}, f32[2,1024]{1,0:T(2,128)}, bf16[3,1024,2048]{2,1,0:T(8,128)(2,1)}) custom-call(bf16[2,128,2048]{2,1,0:T(8,128)(2,1)S(1)} %copy-done, bf16[2,128,2048]{2,1,0:T(8,128)(2,1)S(1)} %copy-done.1, f32[2,128,1024]{2,1,0:T(8,128)S(1)} %pad_maximum_fusion.1.a_ref, bf16[3,1024,2048]{2,1,0:T(8,128)(2,1)} %w_ref.1), custom_call_target="tpu_custom_call" | custom-call | tf_op jit(solution)/shard_map/backward/pallas_call | solution.py:253
Async XLA Ops:
  22.8 7.4 %copy-start.2 = (bf16[3,1024,2048]{2,1,0:T(8,128)(2,1)S(1)}, bf16[3,1024,2048]{2,1,0:T(8,128)(2,1)}, u32[]{:S(2)}) copy-start(bf16[3,1024,2048]{2,1,0:T(8,128)(2,1)} %w_ref.1) | copy-start | bytes 37748740
  31.7 31.6 %copy-start = (bf16[2,128,2048]{2,1,0:T(8,128)(2,1)S(1)}, bf16[2,128,2048]{2,1,0:T(8,128)(2,1)}, u32[]{:S(2)}) copy-start(bf16[2,128,2048]{2,1,0:T(8,128)(2,1)} %gather_inputs.1.x_ref) | copy-start | bytes 3145732
  63.3 1.2 %copy-start.1 = (bf16[2,128,2048]{2,1,0:T(8,128)(2,1)S(1)}, bf16[2,128,2048]{2,1,0:T(8,128)(2,1)}, u32[]{:S(2)}) copy-start(bf16[2,128,2048]{2,1,0:T(8,128)(2,1)} %reduce_errors.1.e_ref) | copy-start | bytes 3145732

commit v2 on v1

v2 whole, which is shorter than its diff:
```python
import functools
import math

import jax
import jax.numpy as jnp
from jax import lax
from jax.experimental import pallas as pl
from jax.experimental.pallas import tpu as pltpu
from jax.sharding import PartitionSpec as P

BF = jnp.bfloat16
F32 = jnp.float32


def place(n):
    me = lax.axis_index("feat")
    return me // 4, (me // 2) % 2, me % 2


def index_of(z, y, c):
    return (z * 2 + y) * 2 + c


def near_first(depth):
    return sorted(range(1, depth), key=lambda k: min(k, depth - k))


def greet(n):
    depth = n // 4
    z, y, c = place(n)
    barrier = pltpu.get_barrier_semaphore()
    peers = [index_of(z, y, 1 - c), index_of(z, 1 - y, c)]
    peers += [index_of((z + k) % depth, y, c) for k in range(1, depth)]
    for peer in peers:
        pl.semaphore_signal(
            barrier, inc=1, device_id={"feat": peer}, device_id_type=pl.DeviceIdType.MESH
        )
    pl.semaphore_wait(barrier, len(peers))


def send(src, dst, send_sem, recv_sem, peer):
    return pltpu.make_async_remote_copy(
        src_ref=src,
        dst_ref=dst,
        send_sem=send_sem,
        recv_sem=recv_sem,
        device_id={"feat": peer},
        device_id_type=pl.DeviceIdType.MESH,
    )


def one_hot(ids_ref, rows, held):
    at = lax.broadcasted_iota(jnp.int32, (rows, held), 0)
    ids = jnp.zeros((rows, held), jnp.int32)
    for row in range(rows):
        ids = jnp.where(at == row, ids_ref[row], ids)
    return (ids == lax.broadcasted_iota(jnp.int32, (rows, held), 1)).astype(BF)


class Spread:
    def __init__(self, n, buf, layer, sems, started):
        self.depth = n // 4
        self.buf, self.layer, self.sems, self.started = buf, layer, sems, started
        self.z, self.y, self.c = place(n)
        self.core = index_of(self.z, self.y, 1 - self.c)
        self.side = index_of(self.z, 1 - self.y, self.c)
        self.order = near_first(self.depth)

    def copy(self, chunk, kind, slot, peer):
        ref = self.buf.at[self.layer, chunk]
        at = self.sems[2 * kind].at[self.layer, slot], self.sems[2 * kind + 1].at[self.layer, slot]
        return send(ref, ref, at[0], at[1], peer)

    def go(self, chunk, kind, slot, peer):
        copy = self.copy(chunk, kind, slot, peer)
        copy.start()
        self.started.append(copy)

    def chunk(self, k, y, c):
        return index_of((self.z - k + self.depth) % self.depth, y, c)

    def begin(self):
        mine = self.chunk(0, self.y, self.c)
        for k in reversed(self.order):
            self.go(mine, 0, k, index_of((self.z + k) % self.depth, self.y, self.c))
        self.go(mine, 1, 0, self.side)
        self.go(mine, 2, 0, self.core)

    def along_z(self):
        for k in self.order:
            chunk = self.chunk(k, self.y, self.c)
            self.copy(chunk, 0, k, self.core).wait_recv()
            self.go(chunk, 1, k, self.side)
            self.go(chunk, 2, k, self.core)

    def along_y(self):
        for k in [0] + self.order:
            chunk = self.chunk(k, 1 - self.y, self.c)
            self.copy(chunk, 1, k, self.side).wait_recv()
            self.go(chunk, 2, self.depth + k, self.core)

    def finish(self, out_ref):
        for k in [0] + self.order:
            self.copy(self.chunk(k, self.y, 1 - self.c), 2, k, self.core).wait_recv()
        for k in [0] + self.order:
            chunk = self.chunk(k, 1 - self.y, 1 - self.c)
            self.copy(chunk, 2, self.depth + k, self.core).wait_recv()
        n, rows = self.buf.shape[1:3]
        for i in range(0, n, 2):
            pair = [self.buf[self.layer, j].astype(F32) for j in (i, i + 1)]
            out_ref[self.layer, pl.ds(i * rows, 2 * rows), :] = jnp.concatenate(pair).astype(BF)


class Reduce:
    def __init__(self, n, part, layer, bufs, sems, started):
        self.n, self.depth = n, n // 4
        self.part, self.layer, self.bufs, self.sems, self.started = part, layer, bufs, sems, started
        self.z, self.y, self.c = place(n)
        self.core = index_of(self.z, self.y, 1 - self.c)
        self.side = index_of(self.z, 1 - self.y, self.c)
        self.order = near_first(self.depth)
        self.far = list(reversed(self.order)) + [0]

    def copy(self, kind, slot, peer):
        at = self.layer, slot
        out, into = self.bufs[2 * kind].at[at], self.bufs[2 * kind + 1].at[at]
        return send(out, into, self.sems[2 * kind].at[at], self.sems[2 * kind + 1].at[at], peer)

    def go(self, kind, slot, peer, value):
        self.bufs[2 * kind][self.layer, slot] = value.astype(BF)
        copy = self.copy(kind, slot, peer)
        copy.start()
        self.started.append(copy)

    def got(self, kind, slot, peer):
        self.copy(kind, slot, peer).wait_recv()
        return self.bufs[2 * kind + 1][self.layer, slot].astype(F32)

    def term(self, k, y, c):
        rows = self.part.shape[1] // self.n
        index = index_of((self.z + k) % self.depth, y, c)
        return self.part[self.layer, pl.ds(pl.multiple_of(index * rows, rows), rows), :]

    def to_core(self):
        for j, y in ((0, 1 - self.y), (1, self.y)):
            for k in self.far:
                self.go(0, j * self.depth + k, self.core, self.term(k, y, 1 - self.c))

    def to_y(self):
        for k in self.far:
            value = self.term(k, 1 - self.y, self.c) + self.got(0, k, self.core)
            self.go(1, k, self.side, value)

    def to_z(self):
        for k in self.far:
            total = self.term(k, self.y, self.c) + self.got(0, self.depth + k, self.core)
            total = total + self.got(1, k, self.side)
            if k:
                self.go(2, k, index_of((self.z + k) % self.depth, self.y, self.c), total)
        self.total = total

    def finish(self):
        total = self.total
        for k in self.order:
            total = total + self.got(2, k, self.core)
        return total


def forward_kernel(
    n, pairs, ids_ref, in_ref, goal_ref, bias_ref, enc_hbm, dec_hbm, x_ref, e_ref, a_ref,
    enc_ref, dec_ref, feat_ref, part_ref, xbuf, ebuf, cst, cin, yst, yin, zst, zin,
    enc_sem, dec_sem, *sems
):
    layers, held, width = in_ref.shape
    rows = ids_ref.shape[0]
    features = a_ref.shape[2]
    me = lax.axis_index("feat")
    enc_copies = [
        pltpu.make_async_copy(enc_hbm.at[i], enc_ref.at[i], enc_sem.at[i]) for i in range(layers)
    ]
    dec_copies = [
        pltpu.make_async_copy(dec_hbm.at[i], dec_ref.at[i], dec_sem.at[i])
        for i in range(len(pairs))
    ]
    hot = one_hot(ids_ref, rows, held)
    for layer in range(layers):
        xbuf[layer, me] = jnp.dot(hot, in_ref[layer], preferred_element_type=F32).astype(BF)
    greet(n)
    started = []
    gathers = [Spread(n, xbuf, layer, sems[:6], started) for layer in range(layers)]
    spreads = [Spread(n, ebuf, layer, sems[6:12], started) for layer in range(layers)]
    bufs = (cst, cin, yst, yin, zst, zin)
    reduces = [Reduce(n, part_ref, layer, bufs, sems[12:], started) for layer in range(layers)]
    for gather in gathers:
        gather.begin()
    for copy in enc_copies + dec_copies:
        copy.start()
    targets = [jnp.dot(hot, goal_ref[layer], preferred_element_type=F32) for layer in range(layers)]

    def encode(layer):
        gathers[layer].finish(x_ref)
        enc_copies[layer].wait()
        tile = min(256, features)

        @pl.loop(0, features // tile)
        def _(i):
            cols = pl.ds(pl.multiple_of(i * tile, tile), tile)
            value = jnp.dot(x_ref[layer], enc_ref[layer, :, cols], preferred_element_type=F32)
            value = value + bias_ref[pl.ds(layer, 1), cols]
            a_ref[layer, :, cols] = value
            feat_ref[layer, :, cols] = jnp.maximum(value, 0.0).astype(BF)

    def decode(target):
        mine = [index for index, pair in enumerate(pairs) if pair[1] == target]
        for index in mine:
            dec_copies[index].wait()
        tile = min(256, width)

        @pl.loop(0, width // tile)
        def _(i):
            cols = pl.ds(pl.multiple_of(i * tile, tile), tile)
            part_ref[target, :, cols] = sum(
                jnp.dot(feat_ref[pairs[p][0]], dec_ref[p, :, cols], preferred_element_type=F32)
                for p in mine
            )

        reduces[target].to_core()

    def errors(target):
        value = reduces[target].finish() - targets[target]
        ebuf[target, me] = value.astype(BF)
        spreads[target].begin()

    stages = (
        lambda layer: gathers[layer].along_z(),
        lambda layer: gathers[layer].along_y(),
        encode,
        decode,
        lambda layer: reduces[layer].to_y(),
        lambda layer: reduces[layer].to_z(),
        errors,
        lambda layer: spreads[layer].along_z(),
        lambda layer: spreads[layer].along_y(),
        lambda layer: spreads[layer].finish(e_ref),
    )
    steps = [(stage + 2 * layer, -layer, stage) for layer in range(layers) for stage in range(len(stages))]
    for _, layer, stage in sorted(steps):
        stages[stage](-layer)
    for copy in started:
        copy.wait_send()


def forward(n, pairs, ids, store_inputs, store_targets, enc_weight, enc_bias, dec_weight):
    layers, _, width = store_inputs.shape
    rows = ids.shape[0]
    features = enc_weight.shape[2]
    tokens = n * rows
    depth = n // 4
    dma = pltpu.SemaphoreType.DMA
    chunks = lambda count: pltpu.VMEM((layers, count, rows, width), BF)
    full = jax.ShapeDtypeStruct((layers, tokens, width), BF)
    vmem = pl.BlockSpec(memory_space=pltpu.VMEM)
    kept = pl.BlockSpec(memory_space=pl.ANY)
    one, two = [dma((layers, depth))] * 2, [dma((layers, 2 * depth))] * 2
    return pl.pallas_call(
        functools.partial(forward_kernel, n, pairs),
        out_shape=(full, full, jax.ShapeDtypeStruct((layers, tokens, features), F32)),
        in_specs=[pl.BlockSpec(memory_space=pltpu.SMEM)] + [vmem] * 3 + [kept] * 2,
        out_specs=(vmem,) * 3,
        scratch_shapes=[
            pltpu.VMEM(enc_weight.shape, BF),
            pltpu.VMEM(dec_weight.shape, BF),
            pltpu.VMEM((layers, tokens, features), BF),
            pltpu.VMEM((layers, tokens, width), F32),
        ]
        + [chunks(n)] * 2
        + [chunks(2 * depth)] * 2
        + [chunks(depth)] * 4
        + [dma((layers,)), dma((len(pairs),))]
        + (one + one + two) * 2
        + (two + one + one),
        compiler_params=pltpu.CompilerParams(
            collective_id=0, has_side_effects=True, vmem_limit_bytes=56 * 1024 * 1024
        ),
        name="forward",
    )(ids, store_inputs, store_targets, enc_bias, enc_weight, dec_weight)


def backward_kernel(pairs, scale, x_ref, e_ref, a_ref, w_ref, enc_ref, bias_ref, dec_ref, xt):
    layers = x_ref.shape[0]

    @pl.when(pl.program_id(0) == 0)
    def _():
        for layer in range(layers):
            xt[layer] = x_ref[layer].T

    for source in range(layers):
        active = a_ref[source]
        turned = jnp.maximum(active, 0.0).astype(BF).T
        grad = None
        for index, (first, target) in enumerate(pairs):
            if first != source:
                continue
            dec = jnp.dot(turned, e_ref[target], preferred_element_type=F32)
            dec_ref[index] = (scale * dec).astype(BF)
            back = lax.dot_general(
                e_ref[target], w_ref[index], (((1,), (1,)), ((), ())), preferred_element_type=F32
            )
            grad = back if grad is None else grad + back
        pre = jnp.where(active > 0, grad, 0.0) * scale
        bias_ref[pl.ds(source, 1), :] = jnp.sum(pre, axis=0, keepdims=True)
        enc = jnp.dot(xt[source], pre.astype(BF), preferred_element_type=F32)
        enc_ref[source] = enc.astype(BF)


def backward(pairs, scale, x, errors, preact, dec_weight):
    layers, tokens, width = x.shape
    features = preact.shape[2]
    tile = min(256, features)
    whole = pl.BlockSpec((layers, tokens, width), lambda i: (0, 0, 0))
    rows = pl.BlockSpec((len(pairs), tile, width), lambda i: (0, i, 0))
    return pl.pallas_call(
        functools.partial(backward_kernel, pairs, scale),
        grid=(features // tile,),
        out_shape=(
            jax.ShapeDtypeStruct((layers, width, features), BF),
            jax.ShapeDtypeStruct((layers, features), F32),
            jax.ShapeDtypeStruct((len(pairs), features, width), BF),
        ),
        in_specs=[whole, whole, pl.BlockSpec((layers, tokens, tile), lambda i: (0, 0, i)), rows],
        out_specs=(
            pl.BlockSpec((layers, width, tile), lambda i: (0, 0, i)),
            pl.BlockSpec((layers, tile), lambda i: (0, i)),
            rows,
        ),
        scratch_shapes=[pltpu.VMEM((layers, width, tokens), BF)],
        compiler_params=pltpu.CompilerParams(vmem_limit_bytes=48 * 1024 * 1024),
        name="backward",
    )(x, errors, preact, dec_weight)


def local(n, store_inputs, store_targets, row_ids, enc_weight, enc_bias, dec_weight):
    layers, width = enc_weight.shape[:2]
    rows = row_ids.shape[0]
    pairs = [(source, target) for source in range(layers) for target in range(source, layers)]
    scale = 1.0 / math.sqrt(rows * n)
    x, errors, preact = forward(
        n, pairs, row_ids, store_inputs, store_targets, enc_weight, enc_bias, dec_weight
    )
    return backward(pairs, scale, x, errors, preact, dec_weight)


def solution(mesh):
    in_specs = (
        P(None, ("group", "feat"), None),
        P(None, ("group", "feat"), None),
        P(("group", "feat")),
        P(None, None, "feat"),
        P(None, "feat"),
        P(None, "feat", None),
    )
    out_specs = (P("group", None, "feat"), P("group", "feat"), P("group", "feat", None))
    body = functools.partial(local, mesh.shape["feat"])
    return jax.shard_map(body, mesh=mesh, in_specs=in_specs, out_specs=out_specs, check_vma=False)
```

time: 84.2 us -> 73.8 us (0.88)
  matrix products: 9.02 us -> 0 us
  other arithmetic: 1.53 us -> 0 us
    dot_general x5 -> x0, matrix products: 9.02 us -> none  [the longest x2 6.8 us: local(): jnp.dot(x[layer], enc_weight[layer], preferred_element_type=F32)]
    unnamed x6, local copies, waits for them, and re-layouts: 1.73 us -> 3.67 us
    another operation x2 -> x0, other arithmetic: 1.53 us -> none  [the longest x1 1.46 us: local(): part = jnp.stack(part).reshape(layers, n, rows, width)]
    reshape x1 -> x0, local copies, waits for them, and re-layouts: 1.32 us -> none  [local(): ids = row_ids.reshape(rows, 1)]
    pallas_call x2 -> x1, Pallas kernels: 49.4 us -> 49.8 us  [forward(): pl.pallas_call(functools.partial(forward_kernel, n, pairs), out_shape=(fu...]
where the time goes in v2:
time: 73.8 us; the launch traced here: 73.4 us
  Pallas kernels  69.1 us (94%)
  local copies, waits for them, and re-layouts  3.67 us (5%)
    pallas_call x1, Pallas kernels, forward(): pl.pallas_call(functools.partial(forward_kernel, n, pairs), out_shape=(fu...  49.8 us
    pallas_call x1, Pallas kernels, backward(): pl.pallas_call(functools.partial(backward_kernel, pairs, scale), grid=(fe...  19.3 us
    unnamed x6, local copies, waits for them, and re-layouts  3.67 us

profile of v2, /device:TPU:0, one launch (start us, length us, event | category | flops | bytes accessed | tf_op | source)
XLA Modules:
  0.0 73.4 jit_solution(8310161149414539896)
XLA Ops:
  0.6 49.8 %forward.1 = (bf16[2,128,2048]{2,1,0:T(8,128)(2,1)}, bf16[2,128,2048]{2,1,0:T(8,128)(2,1)}, f32[2,128,1024]{2,1,0:T(8,128)}) custom-call(s32[8]{0:T(128)} %ids_ref.1, bf16[2,16,2048]{2,1,0:T(8,128)(2,1)} %in_ref.1, bf16[2,16,2048]{2,1,0:T(8,128)(2,1)} %goal_ref.1, f32[2,1024]{1,0:T(2,128)} %bias_ref.1, bf16[2,2048,1024]{2,1,0:T(8,128)(2,1)} %enc_hbm.1, ...), custom_call_target="tpu_custom_call" | custom-call | tf_op jit(solution)/shard_map/forward/pallas_call | solution.py:265
  50.4 0.0 copy-start
  50.4 1.2 %copy-done = bf16[2,128,2048]{2,1,0:T(8,128)(2,1)S(1)} copy-done((bf16[2,128,2048]{2,1,0:T(8,128)(2,1)S(1)}, bf16[2,128,2048]{2,1,0:T(8,128)(2,1)}, u32[]{:S(2)}) %copy-start) | copy-done | bytes 1048600
  51.6 0.0 copy-start.1
  51.6 1.2 %copy-done.1 = bf16[2,128,2048]{2,1,0:T(8,128)(2,1)S(1)} copy-done((bf16[2,128,2048]{2,1,0:T(8,128)(2,1)S(1)}, bf16[2,128,2048]{2,1,0:T(8,128)(2,1)}, u32[]{:S(2)}) %copy-start.1) | copy-done | bytes 1048600
  52.8 0.0 copy-start.2
  52.8 1.2 %copy-done.2 = f32[2,128,1024]{2,1,0:T(8,128)S(1)} copy-done((f32[2,128,1024]{2,1,0:T(8,128)S(1)}, f32[2,128,1024]{2,1,0:T(8,128)}, u32[]{:S(2)}) %copy-start.2) | copy-done | bytes 1048600
  54.1 19.3 %backward.1 = (bf16[2,2048,1024]{2,1,0:T(8,128)(2,1)}, f32[2,1024]{1,0:T(2,128)}, bf16[3,1024,2048]{2,1,0:T(8,128)(2,1)}) custom-call(bf16[2,128,2048]{2,1,0:T(8,128)(2,1)S(1)} %copy-done, bf16[2,128,2048]{2,1,0:T(8,128)(2,1)S(1)} %copy-done.1, f32[2,128,1024]{2,1,0:T(8,128)S(1)} %copy-done.2, bf16[3,1024,2048]{2,1,0:T(8,128)(2,1)} %w_ref.1), custom_call_target="tpu_custom_call" | custom-call | tf_op jit(solution)/shard_map/backward/pallas_call | solution.py:322
Async XLA Ops:
  50.4 1.2 %copy-start = (bf16[2,128,2048]{2,1,0:T(8,128)(2,1)S(1)}, bf16[2,128,2048]{2,1,0:T(8,128)(2,1)}, u32[]{:S(2)}) copy-start(bf16[2,128,2048]{2,1,0:T(8,128)(2,1)} %get-tuple-element.6.x_ref) | copy-start | bytes 3145732
  51.6 1.2 %copy-start.1 = (bf16[2,128,2048]{2,1,0:T(8,128)(2,1)S(1)}, bf16[2,128,2048]{2,1,0:T(8,128)(2,1)}, u32[]{:S(2)}) copy-start(bf16[2,128,2048]{2,1,0:T(8,128)(2,1)} %get-tuple-element.7.e_ref) | copy-start | bytes 3145732
  52.8 1.2 %copy-start.2 = (f32[2,128,1024]{2,1,0:T(8,128)S(1)}, f32[2,128,1024]{2,1,0:T(8,128)}, u32[]{:S(2)}) copy-start(f32[2,128,1024]{2,1,0:T(8,128)} %get-tuple-element.8.a_ref) | copy-start | bytes 3145732

commit v3 on v2

--- a/solution.py
+++ b/solution.py
@@ -167,8 +167,8 @@
 
 
 def forward_kernel(
-    n, pairs, ids_ref, in_ref, goal_ref, bias_ref, enc_hbm, dec_hbm, x_ref, e_ref, a_ref,
-    enc_ref, dec_ref, feat_ref, part_ref, xbuf, ebuf, cst, cin, yst, yin, zst, zin,
+    n, pairs, scale, ids_ref, in_ref, goal_ref, bias_ref, enc_hbm, dec_hbm, xt_ref, ft_ref, e_ref,
+    pre_ref, x_ref, a_ref, enc_ref, dec_ref, feat_ref, part_ref, xbuf, ebuf, cst, cin, yst, yin, zst, zin,
     enc_sem, dec_sem, *sems
 ):
     layers, held, width = in_ref.shape
@@ -231,6 +231,32 @@
         ebuf[target, me] = value.astype(BF)
         spreads[target].begin()
 
+    def turn(layer):
+        xt_ref[layer] = x_ref[layer].T
+        ft_ref[layer] = feat_ref[layer].T
+
+    def feature_grad(target):
+        last = target == layers - 1
+        tile = min(256, features)
+
+        @pl.loop(0, features // tile)
+        def _(i):
+            cols = pl.ds(pl.multiple_of(i * tile, tile), tile)
+            for index, (source, goal) in enumerate(pairs):
+                if goal != target:
+                    continue
+                grad = lax.dot_general(
+                    e_ref[target],
+                    dec_ref[index, cols, :],
+                    (((1,), (1,)), ((), ())),
+                    preferred_element_type=F32,
+                )
+                if source < target:
+                    grad = pre_ref[source, :, cols] + grad
+                if last:
+                    grad = jnp.where(a_ref[source, :, cols] > 0, grad, 0.0) * scale
+                pre_ref[source, :, cols] = grad
+
     stages = (
         lambda layer: gathers[layer].along_z(),
         lambda layer: gathers[layer].along_y(),
@@ -243,14 +269,20 @@
         lambda layer: spreads[layer].along_y(),
         lambda layer: spreads[layer].finish(e_ref),
     )
-    steps = [(stage + 2 * layer, -layer, stage) for layer in range(layers) for stage in range(len(stages))]
-    for _, layer, stage in sorted(steps):
-        stages[stage](-layer)
+    steps = [
+        (stage + 2 * layer, -layer, run)
+        for layer in range(layers)
+        for stage, run in enumerate(stages)
+    ]
+    steps += [(2 * layers + 4.5, -layer, turn) for layer in range(layers)]
+    steps += [(10.5 + 2 * layer, -layer, feature_grad) for layer in range(layers)]
+    for _, layer, run in sorted(steps, key=lambda step: step[:2]):
+        run(-layer)
     for copy in started:
         copy.wait_send()
 
 
-def forward(n, pairs, ids, store_inputs, store_targets, enc_weight, enc_bias, dec_weight):
+def forward(n, pairs, scale, ids, store_inputs, store_targets, enc_weight, enc_bias, dec_weight):
     layers, _, width = store_inputs.shape
     rows = ids.shape[0]
     features = enc_weight.shape[2]
@@ -263,11 +295,18 @@
     kept = pl.BlockSpec(memory_space=pl.ANY)
     one, two = [dma((layers, depth))] * 2, [dma((layers, 2 * depth))] * 2
     return pl.pallas_call(
-        functools.partial(forward_kernel, n, pairs),
-        out_shape=(full, full, jax.ShapeDtypeStruct((layers, tokens, features), F32)),
+        functools.partial(forward_kernel, n, pairs, scale),
+        out_shape=(
+            jax.ShapeDtypeStruct((layers, width, tokens), BF),
+            jax.ShapeDtypeStruct((layers, features, tokens), BF),
+            full,
+            jax.ShapeDtypeStruct((layers, tokens, features), F32),
+        ),
         in_specs=[pl.BlockSpec(memory_space=pltpu.SMEM)] + [vmem] * 3 + [kept] * 2,
-        out_specs=(vmem,) * 3,
+        out_specs=(vmem,) * 4,
         scratch_shapes=[
+            pltpu.VMEM((layers, tokens, width), BF),
+            pltpu.VMEM((layers, tokens, features), F32),
             pltpu.VMEM(enc_weight.shape, BF),
             pltpu.VMEM(dec_weight.shape, BF),
             pltpu.VMEM((layers, tokens, features), BF),
@@ -286,57 +325,51 @@
     )(ids, store_inputs, store_targets, enc_bias, enc_weight, dec_weight)
 
 
-def backward_kernel(pairs, scale, x_ref, e_ref, a_ref, w_ref, enc_ref, bias_ref, dec_ref, xt):
-    layers = x_ref.shape[0]
+def backward_kernel(pairs, scale, xt_ref, ft_ref, e_ref, pre_ref, enc_ref, bias_ref, dec_ref, half):
+    layers = xt_ref.shape[0]
 
     @pl.when(pl.program_id(0) == 0)
     def _():
         for layer in range(layers):
-            xt[layer] = x_ref[layer].T
-
-    for source in range(layers):
-        active = a_ref[source]
-        turned = jnp.maximum(active, 0.0).astype(BF).T
-        grad = None
-        for index, (first, target) in enumerate(pairs):
-            if first != source:
-                continue
-            dec = jnp.dot(turned, e_ref[target], preferred_element_type=F32)
-            dec_ref[index] = (scale * dec).astype(BF)
-            back = lax.dot_general(
-                e_ref[target], w_ref[index], (((1,), (1,)), ((), ())), preferred_element_type=F32
-            )
-            grad = back if grad is None else grad + back
-        pre = jnp.where(active > 0, grad, 0.0) * scale
-        bias_ref[pl.ds(source, 1), :] = jnp.sum(pre, axis=0, keepdims=True)
-        enc = jnp.dot(xt[source], pre.astype(BF), preferred_element_type=F32)
-        enc_ref[source] = enc.astype(BF)
-
-
-def backward(pairs, scale, x, errors, preact, dec_weight):
-    layers, tokens, width = x.shape
-    features = preact.shape[2]
-    tile = min(256, features)
-    whole = pl.BlockSpec((layers, tokens, width), lambda i: (0, 0, 0))
-    rows = pl.BlockSpec((len(pairs), tile, width), lambda i: (0, i, 0))
+            pre = pre_ref[layer]
+            bias_ref[pl.ds(layer, 1), :] = jnp.sum(pre, axis=0, keepdims=True)
+            half[layer] = pre.astype(BF)
+
+    for index, (source, target) in enumerate(pairs):
+        dec = jnp.dot(ft_ref[source], e_ref[target], preferred_element_type=F32)
+        dec_ref[index] = (scale * dec).astype(BF)
+    for layer in range(layers):
+        enc = jnp.dot(xt_ref[layer], half[layer], preferred_element_type=F32)
+        enc_ref[layer] = enc.astype(BF)
+
+
+def backward(pairs, scale, xt, ft, errors, pre):
+    layers, tokens, width = errors.shape
+    features = pre.shape[2]
+    steps = 4
+    rows, tall = features // steps, width // steps
+    tiles = lambda count, high, wide: pl.BlockSpec((count, high, wide), lambda i: (0, i, 0))
+    whole = lambda wide: pl.BlockSpec((layers, tokens, wide), lambda i: (0, 0, 0))
     return pl.pallas_call(
         functools.partial(backward_kernel, pairs, scale),
-        grid=(features // tile,),
+        grid=(steps,),
         out_shape=(
             jax.ShapeDtypeStruct((layers, width, features), BF),
             jax.ShapeDtypeStruct((layers, features), F32),
             jax.ShapeDtypeStruct((len(pairs), features, width), BF),
         ),
-        in_specs=[whole, whole, pl.BlockSpec((layers, tokens, tile), lambda i: (0, 0, i)), rows],
+        in_specs=[
+            tiles(layers, tall, tokens), tiles(layers, rows, tokens), whole(width), whole(features)
+        ],
         out_specs=(
-            pl.BlockSpec((layers, width, tile), lambda i: (0, 0, i)),
-            pl.BlockSpec((layers, tile), lambda i: (0, i)),
-            rows,
+            tiles(layers, tall, features),
+            pl.BlockSpec((layers, features), lambda i: (0, 0)),
+            tiles(len(pairs), rows, width),
         ),
-        scratch_shapes=[pltpu.VMEM((layers, width, tokens), BF)],
-        compiler_params=pltpu.CompilerParams(vmem_limit_bytes=48 * 1024 * 1024),
+        scratch_shapes=[pltpu.VMEM((layers, tokens, features), BF)],
+        compiler_params=pltpu.CompilerParams(vmem_limit_bytes=67_043_328),
         name="backward",
-    )(x, errors, preact, dec_weight)
+    )(xt, ft, errors, pre)
 
 
 def local(n, store_inputs, store_targets, row_ids, enc_weight, enc_bias, dec_weight):
@@ -344,10 +377,8 @@
     rows = row_ids.shape[0]
     pairs = [(source, target) for source in range(layers) for target in range(source, layers)]
     scale = 1.0 / math.sqrt(rows * n)
-    x, errors, preact = forward(
-        n, pairs, row_ids, store_inputs, store_targets, enc_weight, enc_bias, dec_weight
-    )
-    return backward(pairs, scale, x, errors, preact, dec_weight)
+    args = row_ids, store_inputs, store_targets, enc_weight, enc_bias, dec_weight
+    return backward(pairs, scale, *forward(n, pairs, scale, *args))
 
 
 def solution(mesh):

time: 73.8 us -> 66.4 us (0.90)
  local copies, waits for them, and re-layouts: 3.67 us -> 0 us
  Pallas kernels: 69.1 us -> 65.6 us
    unnamed x6 -> x0, local copies, waits for them, and re-layouts: 3.67 us -> none
    pallas_call x2, Pallas kernels: 69.1 us -> 65.6 us  [the longest x1 54.5 us: forward(): pl.pallas_call(functools.partial(forward_kernel, n, pairs, scale), out_sh...]
where the time goes in v3:
time: 66.4 us; the launch traced here: 66.3 us
  Pallas kernels  65.6 us (99%)
    pallas_call x1, Pallas kernels, forward(): pl.pallas_call(functools.partial(forward_kernel, n, pairs, scale), out_sh...  54.5 us
    pallas_call x1, Pallas kernels, backward(): pl.pallas_call(functools.partial(backward_kernel, pairs, scale), grid=(st...  11.2 us

profile of v3, /device:TPU:0, one launch (start us, length us, event | category | flops | bytes accessed | tf_op | source)
XLA Modules:
  0.0 66.3 jit_solution(4587734741699368733)
XLA Ops:
  0.6 54.5 %forward.1 = (bf16[2,2048,128]{2,1,0:T(8,128)(2,1)}, bf16[2,1024,128]{2,1,0:T(8,128)(2,1)}, bf16[2,128,2048]{2,1,0:T(8,128)(2,1)}, f32[2,128,1024]{2,1,0:T(8,128)}) custom-call(s32[8]{0:T(128)} %ids_ref.1, bf16[2,16,2048]{2,1,0:T(8,128)(2,1)} %in_ref.1, bf16[2,16,2048]{2,1,0:T(8,128)(2,1)} %goal_ref.1, f32[2,1024]{1,0:T(2,128)} %bias_ref.1, ...), custom_call_target="tpu_custom_call" | custom-call | tf_op jit(solution)/shard_map/forward/pallas_call | solution.py:297
  55.1 11.2 %backward.1 = (bf16[2,2048,1024]{2,1,0:T(8,128)(2,1)}, f32[2,1024]{1,0:T(2,128)}, bf16[3,1024,2048]{2,1,0:T(8,128)(2,1)}) custom-call(bf16[2,2048,128]{2,1,0:T(8,128)(2,1)} %get-tuple-element.7.xt_ref, bf16[2,1024,128]{2,1,0:T(8,128)(2,1)} %get-tuple-element.8.ft_ref, bf16[2,128,2048]{2,1,0:T(8,128)(2,1)} %get-tuple-element.9.e_ref, ...), custom_call_target="tpu_custom_call" | custom-call | tf_op jit(solution)/shard_map/backward/pallas_call | solution.py:353

commit v4 on v3

--- a/solution.py
+++ b/solution.py
@@ -200,7 +200,7 @@
     def encode(layer):
         gathers[layer].finish(x_ref)
         enc_copies[layer].wait()
-        tile = min(256, features)
+        tile = min(512, features)
 
         @pl.loop(0, features // tile)
         def _(i):
@@ -214,7 +214,7 @@
         mine = [index for index, pair in enumerate(pairs) if pair[1] == target]
         for index in mine:
             dec_copies[index].wait()
-        tile = min(256, width)
+        tile = min(512, width)
 
         @pl.loop(0, width // tile)
         def _(i):
@@ -237,7 +237,7 @@
 
     def feature_grad(target):
         last = target == layers - 1
-        tile = min(256, features)
+        tile = min(512, features)
 
         @pl.loop(0, features // tile)
         def _(i):
@@ -270,12 +270,12 @@
         lambda layer: spreads[layer].finish(e_ref),
     )
     steps = [
-        (stage + 2 * layer, -layer, run)
+        (stage + layer, -layer, run)
         for layer in range(layers)
         for stage, run in enumerate(stages)
     ]
-    steps += [(2 * layers + 4.5, -layer, turn) for layer in range(layers)]
-    steps += [(10.5 + 2 * layer, -layer, feature_grad) for layer in range(layers)]
+    steps += [(layers + 5.5, -layer, turn) for layer in range(layers)]
+    steps += [(9.5 + layer, -layer, feature_grad) for layer in range(layers)]
     for _, layer, run in sorted(steps, key=lambda step: step[:2]):
         run(-layer)
     for copy in started:

time: 66.4 us -> 62.6 us (0.943)
  Pallas kernels: 65.6 us -> 61.8 us
    pallas_call x1, Pallas kernels: 54.5 us -> 50.6 us  [forward(): pl.pallas_call(functools.partial(forward_kernel, n, pairs, scale), out_sh...]
where the time goes in v4:
time: 62.6 us; the launch traced here: 62.4 us
  Pallas kernels  61.8 us (99%)
  between operations  0.64 us (1%)
    pallas_call x1, Pallas kernels, forward(): pl.pallas_call(functools.partial(forward_kernel, n, pairs, scale), out_sh...  50.6 us
    pallas_call x1, Pallas kernels, backward(): pl.pallas_call(functools.partial(backward_kernel, pairs, scale), grid=(st...  11.2 us

profile of v4, /device:TPU:0, one launch (start us, length us, event | category | flops | bytes accessed | tf_op | source)
XLA Modules:
  0.0 62.4 jit_solution(6904664399713790920)
XLA Ops:
  0.6 50.6 %forward.1 = (bf16[2,2048,128]{2,1,0:T(8,128)(2,1)}, bf16[2,1024,128]{2,1,0:T(8,128)(2,1)}, bf16[2,128,2048]{2,1,0:T(8,128)(2,1)}, f32[2,128,1024]{2,1,0:T(8,128)}) custom-call(s32[8]{0:T(128)} %ids_ref.1, bf16[2,16,2048]{2,1,0:T(8,128)(2,1)} %in_ref.1, bf16[2,16,2048]{2,1,0:T(8,128)(2,1)} %goal_ref.1, f32[2,1024]{1,0:T(2,128)} %bias_ref.1, ...), custom_call_target="tpu_custom_call" | custom-call | tf_op jit(solution)/shard_map/forward/pallas_call | solution.py:297
  51.3 11.2 %backward.1 = (bf16[2,2048,1024]{2,1,0:T(8,128)(2,1)}, f32[2,1024]{1,0:T(2,128)}, bf16[3,1024,2048]{2,1,0:T(8,128)(2,1)}) custom-call(bf16[2,2048,128]{2,1,0:T(8,128)(2,1)} %get-tuple-element.7.xt_ref, bf16[2,1024,128]{2,1,0:T(8,128)(2,1)} %get-tuple-element.8.ft_ref, bf16[2,128,2048]{2,1,0:T(8,128)(2,1)} %get-tuple-element.9.e_ref, ...), custom_call_target="tpu_custom_call" | custom-call | tf_op jit(solution)/shard_map/backward/pallas_call | solution.py:353
